TPU v7x, 512 devices: a whole 4x8x8 slice. The times are simulated.
512 devices in a mesh: tile: 32 (over x, z), row: 16 (over y, core).
Axes of the slice: x: 4, y: 8, z: 8, core: 2. Of those that a mesh axis runs over, the one named last changes fastest.
Arguments:
- voltage: float32 [32, 16, 1, 64, 128], P('tile', 'row'), may hold values from -6 to 6
- history: bfloat16 [32, 16, 32, 64, 128], P('tile', 'row'), may hold values from -6 to 6
- far_blocks: bfloat16 [32, 16, 32, 128, 128], P('tile', 'row'), may hold values from -0.09375 to 0.09375
- far_target: int32 [32, 16, 32, 1], P('tile', 'row'), may hold values from 0 to 31; in each aligned block of 32 rows (0 to 31, 32 to 63, ..., all dimensions but the last counted through in order) at most 2 rows name the same one
- far_delay: int32 [32, 16, 32], P('tile', 'row'), may hold values from 1 to 32
- near_blocks: bfloat16 [32, 16, 3, 128, 128], P('tile', 'row'), may hold values from -0.15625 to 0.15625
- near_link: int32 [32, 16, 2], P('tile', 'row'), may hold values 0 or 1
- jacobi_blocks: bfloat16 [32, 16, 128, 128], P('tile', 'row'), may hold values from -0.21875 to 0.21875
Outputs:
- currents: float32 [32, 16, 1, 64, 128], P('tile', 'row')
Inputs may be any that keep to these rules, and one draw needn't show every extreme that they name: `far_target`: among the 32 entries of one tile at most 2 name the same target, and some tile has exactly 2 naming one target.
All inputs are finite; a program needn't handle non-finite values. No bound on the sum of `near_link` on one device may be relied on, other than what follows from the above.
Results may differ from a plain program's by a relative error of at most 0.0003.
Values sent between devices are 32-bit elements; how exact they have to be, the bound alone decides.
No kernel may reach another device: no remote copies, remote signals or barrier semaphores. Data moves between devices by JAX's collectives and lax.ppermute only.
A program may use at most 64 MiB of HBM per device.

v0:
```python
import jax
import jax.numpy as jnp
from jax import lax
from jax.sharding import PartitionSpec as P

ITERS = 5
PRECISE = lax.Precision.HIGHEST


def padded_2(array, sides, width):
    for axis, dim in sides:
        size, length = (lax.axis_size(axis), array.shape[dim])
        up = [(i, (i + 1) % size) for i in range(size - 1)]
        down = [(j, i) for i, j in up]
        last = lax.slice_in_dim(array, length - width, length, axis=dim)
        first = lax.slice_in_dim(array, 0, width, axis=dim)
        before = lax.ppermute(last, axis, up)
        after = lax.ppermute(first, axis, down)
        array = jnp.concatenate([before, array, after], axis=dim)
    return array


def near_apply(field, near_f32, link_gain):
    padded = padded_2(field[None], (("row", 0),), 1)
    result = field + jnp.dot(field, near_f32[1], precision=PRECISE)
    result = result + link_gain[0] * jnp.dot(padded[0], near_f32[0], precision=PRECISE)
    result = result + link_gain[1] * jnp.dot(padded[2], near_f32[2], precision=PRECISE)
    return result


def jacobi_apply(field, jacobi_f32):
    return field + jnp.dot(field, jacobi_f32, precision=PRECISE)


def givens_solve(hessen, start_norm, iterations):
    matrix = [[hessen[i][k] for k in range(iterations)] for i in range(iterations + 1)]
    target = [start_norm] + [jnp.zeros_like(start_norm) for k in range(iterations)]
    for j in range(iterations):
        diag_val = matrix[j][j]
        below_val = matrix[j + 1][j]
        radius = jnp.sqrt(diag_val * diag_val + below_val * below_val)
        cosine = diag_val / radius
        sine_val = below_val / radius
        for k in range(j, iterations):
            upper_val = matrix[j][k]
            lower_val = matrix[j + 1][k]
            matrix[j][k] = cosine * upper_val + sine_val * lower_val
            matrix[j + 1][k] = cosine * lower_val - sine_val * upper_val
        target[j + 1] = -sine_val * target[j]
        target[j] = cosine * target[j]
    coeffs = [None] * iterations
    for j in reversed(range(iterations)):
        partial_val = target[j]
        for k in range(j + 1, iterations):
            partial_val = partial_val - matrix[j][k] * coeffs[k]
        coeffs[j] = partial_val / matrix[j][j]
    return coeffs


def krylov_solve(right_side, near_f32, link_gain, jacobi_f32):
    initial = jacobi_apply(right_side, jacobi_f32)
    start_sq = lax.psum(jnp.sum(initial * initial, axis=1), ("tile", "row"))
    start_norm = jnp.sqrt(start_sq)
    basis = [initial / start_norm[:, None]]
    zero_row = jnp.zeros_like(start_norm)
    hessen = [[zero_row for k in range(ITERS)] for i in range(ITERS + 1)]
    for j in range(ITERS):
        candidate = jacobi_apply(near_apply(basis[j], near_f32, link_gain), jacobi_f32)
        local_dots = jnp.stack([jnp.sum(v * candidate, axis=1) for v in basis])
        projections = lax.psum(local_dots, ("tile", "row"))
        for i in range(j + 1):
            candidate = candidate - projections[i][:, None] * basis[i]
        new_sq = lax.psum(jnp.sum(candidate * candidate, axis=1), ("tile", "row"))
        new_norm = jnp.sqrt(new_sq)
        for i in range(j + 1):
            hessen[i][j] = projections[i]
        hessen[j + 1][j] = new_norm
        basis.append(candidate / new_norm[:, None])
    coeffs = givens_solve(hessen, start_norm, ITERS)
    result = coeffs[0][:, None] * basis[0]
    for j in range(1, ITERS):
        result = result + coeffs[j][:, None] * basis[j]
    return result


def per_device(
    voltage, history, far_blocks, far_target, far_delay, near_blocks, near_link, jacobi_blocks
):
    voltage = voltage[0, 0]
    history = history[0, 0]
    far_blocks = far_blocks[0, 0]
    targets = far_target[0, 0, :, 0]
    delays = far_delay[0, 0]
    near_f32 = near_blocks[0, 0].astype(jnp.float32)
    link_gain = near_link[0, 0].astype(jnp.float32)
    jacobi_f32 = jacobi_blocks[0, 0].astype(jnp.float32)
    tile_count = lax.axis_size("tile")
    entries = far_blocks.shape[0]
    capacity = max(2, entries // tile_count + 1)
    scenarios = voltage.shape[1]
    segments = voltage.shape[2]
    ordinal = jnp.arange(entries, dtype=jnp.int32)
    earlier = (ordinal[:, None] > ordinal[None, :]) & (targets[:, None] == targets[None, :])
    ranking = jnp.sum(earlier.astype(jnp.int32), axis=1)
    destination = targets * capacity + ranking
    placing = (
        jnp.arange(tile_count * capacity, dtype=jnp.int32)[:, None] == destination[None, :]
    ).astype(jnp.float32)
    currents = []
    pieces = [c.astype(jnp.bfloat16)[None] for c in reversed(currents)]
    stacked = jnp.concatenate(pieces + [history], axis=0)
    chosen = jnp.take(stacked, delays - 1, axis=0)
    products = jnp.einsum("lcs,lst->lct", chosen, far_blocks, preferred_element_type=jnp.float32)
    flattened = products.reshape(entries, scenarios * segments)
    bucket = jnp.dot(placing, flattened, precision=PRECISE).reshape(
        tile_count, capacity, scenarios, segments
    )
    received = lax.all_to_all(bucket, "tile", split_axis=0, concat_axis=0, tiled=True)
    far_field = jnp.sum(received, axis=(0, 1))
    right_side = voltage[0] - far_field
    currents.append(krylov_solve(right_side, near_f32, link_gain, jacobi_f32))
    return jnp.stack(currents)[None, None]


def solution(mesh):
    return jax.shard_map(
        per_device,
        mesh=mesh,
        in_specs=(
            P("tile", "row", None, None, None),
            P("tile", "row", None, None, None),
            P("tile", "row", None, None, None),
            P("tile", "row", None, None),
            P("tile", "row", None),
            P("tile", "row", None, None, None),
            P("tile", "row", None),
            P("tile", "row", None, None),
        ),
        out_specs=P("tile", "row", None, None, None),
        check_vma=False,
    )
```

profile of v0, /device:TPU:1, one launch (start us, length us, event | category | flops | bytes accessed | tf_op | source)
XLA Modules:
  0.0 1178.2 jit_solution(18012329410993611256)
XLA Ops:
  6.9 2.6 copy.13
  9.4 13.8 %all-to-all-start = ((f32[32,2,64,128]{3,2,1,0:T(8,128)}), f32[32,2,64,128]{3,2,1,0:T(8,128)S(1)}, u32[]{:S(2)}, u32[]{:S(2)}) async-start(f32[32,2,64,128]{3,2,1,0:T(8,128)} %copy.13), calls=%async_computation | async-start | bytes 4194304 | tf_op jit(solution)/shard_map/all_to_all | solution.py:118
  23.9 48.2 %all-to-all-done = f32[32,2,64,128]{3,2,1,0:T(8,128)S(1)} async-done(((f32[32,2,64,128]{3,2,1,0:T(8,128)}), f32[32,2,64,128]{3,2,1,0:T(8,128)S(1)}, u32[]{:S(2)}, u32[]{:S(2)}) %all-to-all-start) | async-done | bytes 2097184 | tf_op jit(solution)/shard_map/all_to_all | solution.py:118
  72.6 98.6 %psum.77 = f32[64]{0:T(128)S(1)} all-reduce(f32[64]{0:T(128)S(1)} %get-tuple-element.55), channel_id=1, replica_groups=mesh['tile'=32,'row'=16] {'tile','row'}, use_global_device_ids=true, to_apply=%region_3.4 | all-reduce | flops 64 | bytes 512 | tf_op jit(solution)/shard_map/psum | solution.py:62
  171.3 3.0 collective-permute-start
  177.2 2.3 collective-permute-done.1
  180.5 95.9 %psum.78 = f32[64]{0:T(128)S(1)} all-reduce(f32[64]{0:T(128)S(1)} %get-tuple-element.57), channel_id=1, replica_groups=mesh['tile'=32,'row'=16] {'tile','row'}, use_global_device_ids=true, to_apply=%region_5.6 | all-reduce | flops 64 | bytes 512 | tf_op jit(solution)/shard_map/psum | solution.py:70
  276.6 95.5 %psum.79 = f32[64]{0:T(128)S(1)} all-reduce(f32[64]{0:T(128)S(1)} %multiply_reduce_fusion.18), channel_id=1, replica_groups=mesh['tile'=32,'row'=16] {'tile','row'}, use_global_device_ids=true, to_apply=%region_7.8 | all-reduce | flops 64 | bytes 512 | tf_op jit(solution)/shard_map/psum | solution.py:73
  372.3 2.7 collective-permute-start.2
  377.9 2.5 collective-permute-done.3
  381.5 95.9 %psum.80 = f32[2,64]{1,0:T(2,128)S(1)} all-reduce(f32[2,64]{1,0:T(2,128)S(1)} %pad_maximum_fusion.2), channel_id=1, replica_groups=mesh['tile'=32,'row'=16] {'tile','row'}, use_global_device_ids=true, to_apply=%region_10.11 | all-reduce | flops 128 | bytes 1024 | tf_op jit(solution)/shard_map/psum | solution.py:70
  477.7 95.3 %psum.81 = f32[64]{0:T(128)S(1)} all-reduce(f32[64]{0:T(128)S(1)} %get-tuple-element.34), channel_id=1, replica_groups=mesh['tile'=32,'row'=16] {'tile','row'}, use_global_device_ids=true, to_apply=%region_12.13 | all-reduce | flops 64 | bytes 512 | tf_op jit(solution)/shard_map/psum | solution.py:73
  573.0 3.3 collective-permute-start.4
  579.3 2.5 collective-permute-done.5
  583.0 96.0 %psum.82 = f32[3,64]{1,0:T(4,128)S(1)} all-reduce(f32[3,64]{1,0:T(4,128)S(1)} %pad_maximum_fusion), channel_id=1, replica_groups=mesh['tile'=32,'row'=16] {'tile','row'}, use_global_device_ids=true, to_apply=%region_16.17 | all-reduce | flops 192 | bytes 1536 | tf_op jit(solution)/shard_map/psum | solution.py:70
  679.2 95.1 %psum.83 = f32[64]{0:T(128)S(1)} all-reduce(f32[64]{0:T(128)S(1)} %get-tuple-element.32), channel_id=1, replica_groups=mesh['tile'=32,'row'=16] {'tile','row'}, use_global_device_ids=true, to_apply=%region_18.19 | all-reduce | flops 64 | bytes 512 | tf_op jit(solution)/shard_map/psum | solution.py:73
  774.6 3.1 collective-permute-start.6
  780.7 2.3 collective-permute-done.7
  784.1 96.8 %psum.84 = f32[4,64]{1,0:T(4,128)S(1)} all-reduce(f32[4,64]{1,0:T(4,128)S(1)} %pad_maximum_fusion.1), channel_id=1, replica_groups=mesh['tile'=32,'row'=16] {'tile','row'}, use_global_device_ids=true, to_apply=%region_23.24 | all-reduce | flops 256 | bytes 2048 | tf_op jit(solution)/shard_map/psum | solution.py:70
  881.1 94.5 %psum.85 = f32[64]{0:T(128)S(1)} all-reduce(f32[64]{0:T(128)S(1)} %get-tuple-element.30), channel_id=1, replica_groups=mesh['tile'=32,'row'=16] {'tile','row'}, use_global_device_ids=true, to_apply=%region_25.26 | all-reduce | flops 64 | bytes 512 | tf_op jit(solution)/shard_map/psum | solution.py:73
  975.7 3.3 collective-permute-start.8
  981.9 2.5 collective-permute-done.9
  985.6 96.2 %psum.86 = f32[5,64]{1,0:T(8,128)S(1)} all-reduce(f32[5,64]{1,0:T(8,128)S(1)} %stack.75), channel_id=1, replica_groups=mesh['tile'=32,'row'=16] {'tile','row'}, use_global_device_ids=true, to_apply=%region_31.32 | all-reduce | flops 320 | bytes 2560 | tf_op jit(solution)/shard_map/psum | solution.py:70
  1082.1 95.2 %psum.87 = f32[64]{0:T(128)S(1)} all-reduce(f32[64]{0:T(128)S(1)} %multiply_reduce_fusion), channel_id=1, replica_groups=mesh['tile'=32,'row'=16] {'tile','row'}, use_global_device_ids=true, to_apply=%region_33.34 | all-reduce | flops 64 | bytes 512 | tf_op jit(solution)/shard_map/psum | solution.py:73
  (80 shorter events, 30.6 us)
Async XLA Ops:
  0.0 4.7 copy-start
  9.4 13.9 %copy-start.4 = (s32[1,1,2]{2,1,0:T(1,128)S(1)}, s32[1,1,2]{2,1,0:T(1,128)}, u32[]{:S(2)}) copy-start(s32[1,1,2]{2,1,0:T(1,128)} %param.14) | copy-start | bytes 28
  9.4 62.7 %all-to-all-start = ((f32[32,2,64,128]{3,2,1,0:T(8,128)}), f32[32,2,64,128]{3,2,1,0:T(8,128)S(1)}, u32[]{:S(2)}, u32[]{:S(2)}) async-start(f32[32,2,64,128]{3,2,1,0:T(8,128)} %copy.13), calls=%async_computation | async-start | bytes 4194304 | tf_op jit(solution)/shard_map/all_to_all | solution.py:118
  23.3 49.0 %copy-start.2 = (f32[1,1,1,64,128]{4,3,2,1,0:T(8,128)S(1)}, f32[1,1,1,64,128]{4,3,2,1,0:T(8,128)}, u32[]{:S(2)}) copy-start(f32[1,1,1,64,128]{4,3,2,1,0:T(8,128)} %param.8) | copy-start | bytes 98308
  23.3 49.0 %copy-start.3 = (bf16[1,1,128,128]{3,2,1,0:T(8,128)(2,1)S(1)}, bf16[1,1,128,128]{3,2,1,0:T(8,128)(2,1)}, u32[]{:S(2)}) copy-start(bf16[1,1,128,128]{3,2,1,0:T(8,128)(2,1)} %param.15) | copy-start | bytes 98308
  23.3 152.8 %copy-start.1 = (bf16[1,1,3,128,128]{4,3,2,1,0:T(8,128)(2,1)S(1)}, bf16[1,1,3,128,128]{4,3,2,1,0:T(8,128)(2,1)}, u32[]{:S(2)}) copy-start(bf16[1,1,3,128,128]{4,3,2,1,0:T(8,128)(2,1)} %param.13) | copy-start | bytes 294916
  171.3 5.1 collective-permute-start
  174.2 5.2 collective-permute-start.1
  372.3 4.8 collective-permute-start.2
  375.2 5.2 collective-permute-start.3
  573.0 5.5 collective-permute-start.4
  576.6 5.2 collective-permute-start.5
  774.6 5.2 collective-permute-start.6
  777.7 5.2 collective-permute-start.7
  975.7 5.4 collective-permute-start.8
  979.2 5.2 collective-permute-start.9
where the time goes:
time: 1180 us
  blocking collectives  1060 us (90%)
  waiting for transfers between devices  60.3 us (5%)
  starting transfers between devices  38.9 us (3%)
  matrix products  12.9 us (1%)
    psum x5, blocking collectives, krylov_solve(): projections = lax.psum(local_dots, ('tile', 'row'))  481 us
    psum x5, blocking collectives, krylov_solve(): new_sq = lax.psum(jnp.sum(candidate * candidate, axis=1), ('tile', 'row'))  476 us
    psum x1, blocking collectives, krylov_solve(): start_sq = lax.psum(jnp.sum(initial * initial, axis=1), ('tile', 'row'))  98.6 us
    all_to_all x1, waiting for transfers between devices, per_device(): lax.all_to_all(bucket, 'tile', split_axis=0, concat_axis=0, tiled=True)  48.2 us
  transfers between devices with their start and end apart: 11, of which 6 were waited for; matrix products, arithmetic and copies ran while one was open for 0% of the time, Pallas kernels for 0%

commit v1 on v0

--- a/solution.py
+++ b/solution.py
@@ -1,3 +1,4 @@
+import functools
 import jax
 import jax.numpy as jnp
 from jax import lax
@@ -5,6 +6,14 @@
 
 ITERS = 5
 PRECISE = lax.Precision.HIGHEST
+
+
+def lay_fields(arr_in, named_axis):
+    everything = lax.all_gather(arr_in, axis_name=named_axis)
+    return jnp.sum(everything, axis=0)
+
+
+object_play = functools.partial(lay_fields, named_axis=("tile", "row"))
 
 
 def padded_2(array, sides, width):
@@ -67,7 +76,7 @@
     for j in range(ITERS):
         candidate = jacobi_apply(near_apply(basis[j], near_f32, link_gain), jacobi_f32)
         local_dots = jnp.stack([jnp.sum(v * candidate, axis=1) for v in basis])
-        projections = lax.psum(local_dots, ("tile", "row"))
+        projections = object_play(local_dots)
         for i in range(j + 1):
             candidate = candidate - projections[i][:, None] * basis[i]
         new_sq = lax.psum(jnp.sum(candidate * candidate, axis=1), ("tile", "row"))

time: 1180 us -> 1250 us (1.059)
  waiting for transfers between devices: 60.3 us -> 318 us
  blocking collectives: 1060 us -> 853 us
  between operations: 0.44 us -> 13.9 us
    psum x5 -> x0, blocking collectives: 481 us -> none  [krylov_solve(): projections = lax.psum(local_dots, ('tile', 'row'))]
    all_gather x0 -> x4, blocking collectives: none -> 279 us  [lay_fields(): everything = lax.all_gather(arr_in, axis_name=named_axis)]
    unnamed x0 -> x2, waiting for transfers between devices: none -> 258 us
  transfers between devices with their start and end apart: 11 -> 12, of which waited for: 6 -> 7; matrix products, arithmetic and copies ran while one was open for 0% -> 0% of each run, Pallas kernels for 0% -> 0%
where the time goes in v1:
time: 1250 us
  blocking collectives  853 us (68%)
  waiting for transfers between devices  318 us (25%)
  starting transfers between devices  40.3 us (3%)
  between operations  13.9 us (1%)
  matrix products  12.9 us (1%)
    psum x5, blocking collectives, krylov_solve(): new_sq = lax.psum(jnp.sum(candidate * candidate, axis=1), ('tile', 'row'))  476 us
    all_gather x4, blocking collectives, lay_fields(): everything = lax.all_gather(arr_in, axis_name=named_axis)  279 us
    unnamed x2, waiting for transfers between devices  258 us
    psum x1, blocking collectives, krylov_solve(): start_sq = lax.psum(jnp.sum(initial * initial, axis=1), ('tile', 'row'))  98.6 us
    all_to_all x1, waiting for transfers between devices, per_device(): lax.all_to_all(bucket, 'tile', split_axis=0, concat_axis=0, tiled=True)  48.2 us
  transfers between devices with their start and end apart: 12, of which 7 were waited for; matrix products, arithmetic and copies ran while one was open for 0% of the time, Pallas kernels for 0%

profile of v1, /device:TPU:1, one launch (start us, length us, event | category | flops | bytes accessed | tf_op | source)
XLA Modules:
  0.0 1253.0 jit_solution(11528460509925113692)
XLA Ops:
  13.4 2.6 copy.13
  16.0 13.8 %all-to-all-start = ((f32[32,2,64,128]{3,2,1,0:T(8,128)}), f32[32,2,64,128]{3,2,1,0:T(8,128)S(1)}, u32[]{:S(2)}, u32[]{:S(2)}) async-start(f32[32,2,64,128]{3,2,1,0:T(8,128)} %copy.13), calls=%async_computation | async-start | bytes 4194304 | tf_op jit(solution)/shard_map/all_to_all | solution.py:127
  30.5 48.2 %all-to-all-done = f32[32,2,64,128]{3,2,1,0:T(8,128)S(1)} async-done(((f32[32,2,64,128]{3,2,1,0:T(8,128)}), f32[32,2,64,128]{3,2,1,0:T(8,128)S(1)}, u32[]{:S(2)}, u32[]{:S(2)}) %all-to-all-start) | async-done | bytes 2097184 | tf_op jit(solution)/shard_map/all_to_all | solution.py:127
  79.1 98.6 %psum.42 = f32[64]{0:T(128)S(1)} all-reduce(f32[64]{0:T(128)S(1)} %get-tuple-element.55), channel_id=1, replica_groups=mesh['tile'=32,'row'=16] {'tile','row'}, use_global_device_ids=true, to_apply=%region_3.4 | all-reduce | flops 64 | bytes 512 | tf_op jit(solution)/shard_map/psum | solution.py:71
  177.8 2.9 collective-permute-start
  183.7 2.3 collective-permute-done.1
  188.1 257.9 %all-reduce.3.cloned.1.call-done = f32[32768]{0:T(1024)} async-done(((f32[32768]{0:T(1024)}), f32[32768]{0:T(1024)}) %all-reduce.3.cloned.1.call-update) | async-done | bytes 131088
  447.2 95.1 %psum.43 = f32[64]{0:T(128)S(1)} all-reduce(f32[64]{0:T(128)S(1)} %multiply_reduce_fusion.18), channel_id=1, replica_groups=mesh['tile'=32,'row'=16] {'tile','row'}, use_global_device_ids=true, to_apply=%region_7.8 | all-reduce | flops 64 | bytes 512 | tf_op jit(solution)/shard_map/psum | solution.py:82
  542.4 3.3 collective-permute-start.2
  548.6 2.5 collective-permute-done.3
  552.3 65.7 %all-gather.5 = f32[512,2,64]{2,1,0:T(2,128)S(1)} all-gather(f32[1,2,64]{2,1,0:T(2,128)S(1)} %maximum_bitcast_fusion.2), channel_id=3, replica_groups=mesh['tile'=32,'row'=16] {'tile','row'}, dimensions={0}, use_global_device_ids=true | all-gather | bytes 262656 | tf_op jit(solution)/shard_map/all_gather | solution.py:12
  618.7 95.5 %psum.44 = f32[64]{0:T(128)S(1)} all-reduce(f32[64]{0:T(128)S(1)} %get-tuple-element.34), channel_id=1, replica_groups=mesh['tile'=32,'row'=16] {'tile','row'}, use_global_device_ids=true, to_apply=%region_12.13 | all-reduce | flops 64 | bytes 512 | tf_op jit(solution)/shard_map/psum | solution.py:82
  714.3 3.2 collective-permute-start.4
  720.5 2.5 collective-permute-done.5
  724.1 72.7 %all-gather.6 = f32[512,3,64]{2,1,0:T(4,128)S(1)} all-gather(f32[1,3,64]{2,1,0:T(4,128)S(1)} %maximum_bitcast_fusion), channel_id=4, replica_groups=mesh['tile'=32,'row'=16] {'tile','row'}, dimensions={0}, use_global_device_ids=true | all-gather | bytes 393984 | tf_op jit(solution)/shard_map/all_gather | solution.py:12
  797.5 95.0 %psum.45 = f32[64]{0:T(128)S(1)} all-reduce(f32[64]{0:T(128)S(1)} %get-tuple-element.32), channel_id=1, replica_groups=mesh['tile'=32,'row'=16] {'tile','row'}, use_global_device_ids=true, to_apply=%region_18.19 | all-reduce | flops 64 | bytes 512 | tf_op jit(solution)/shard_map/psum | solution.py:82
  892.9 3.6 collective-permute-start.6
  899.3 2.5 collective-permute-done.7
  902.9 72.5 %all-gather.7 = f32[512,4,64]{2,1,0:T(4,128)S(1)} all-gather(f32[1,4,64]{2,1,0:T(4,128)S(1)} %maximum_bitcast_fusion.1), channel_id=5, replica_groups=mesh['tile'=32,'row'=16] {'tile','row'}, dimensions={0}, use_global_device_ids=true | all-gather | bytes 525312 | tf_op jit(solution)/shard_map/all_gather | solution.py:12
  976.3 95.0 %psum.46 = f32[64]{0:T(128)S(1)} all-reduce(f32[64]{0:T(128)S(1)} %get-tuple-element.30), channel_id=1, replica_groups=mesh['tile'=32,'row'=16] {'tile','row'}, use_global_device_ids=true, to_apply=%region_25.26 | all-reduce | flops 64 | bytes 512 | tf_op jit(solution)/shard_map/psum | solution.py:82
  1071.4 3.7 collective-permute-start.8
  1078.0 2.5 collective-permute-done.9
  1081.7 67.8 %all-gather.8 = f32[512,5,64]{2,1,0:T(8,128)S(1)} all-gather(f32[1,5,64]{2,1,0:T(8,128)S(1)} %bitcast.320), channel_id=6, replica_groups=mesh['tile'=32,'row'=16] {'tile','row'}, dimensions={0}, use_global_device_ids=true | all-gather | bytes 656640 | tf_op jit(solution)/shard_map/all_gather | solution.py:12
  1150.3 95.0 %psum.47 = f32[64]{0:T(128)S(1)} all-reduce(f32[64]{0:T(128)S(1)} %multiply_reduce_fusion), channel_id=1, replica_groups=mesh['tile'=32,'row'=16] {'tile','row'}, use_global_device_ids=true, to_apply=%region_33.34 | all-reduce | flops 64 | bytes 512 | tf_op jit(solution)/shard_map/psum | solution.py:82
  (92 shorter events, 34.7 us)
Async XLA Ops:
  6.5 4.7 copy-start
  16.0 13.9 %copy-start.5 = (s32[1,1,2]{2,1,0:T(1,128)S(1)}, s32[1,1,2]{2,1,0:T(1,128)}, u32[]{:S(2)}) copy-start(s32[1,1,2]{2,1,0:T(1,128)} %param.14) | copy-start | bytes 28
  16.0 62.7 %all-to-all-start = ((f32[32,2,64,128]{3,2,1,0:T(8,128)}), f32[32,2,64,128]{3,2,1,0:T(8,128)S(1)}, u32[]{:S(2)}, u32[]{:S(2)}) async-start(f32[32,2,64,128]{3,2,1,0:T(8,128)} %copy.13), calls=%async_computation | async-start | bytes 4194304 | tf_op jit(solution)/shard_map/all_to_all | solution.py:127
  29.8 49.0 %copy-start.3 = (f32[1,1,1,64,128]{4,3,2,1,0:T(8,128)S(1)}, f32[1,1,1,64,128]{4,3,2,1,0:T(8,128)}, u32[]{:S(2)}) copy-start(f32[1,1,1,64,128]{4,3,2,1,0:T(8,128)} %param.8) | copy-start | bytes 98308
  29.8 49.0 %copy-start.4 = (bf16[1,1,128,128]{3,2,1,0:T(8,128)(2,1)S(1)}, bf16[1,1,128,128]{3,2,1,0:T(8,128)(2,1)}, u32[]{:S(2)}) copy-start(bf16[1,1,128,128]{3,2,1,0:T(8,128)(2,1)} %param.15) | copy-start | bytes 98308
  29.8 152.8 %copy-start.1 = (bf16[1,1,3,128,128]{4,3,2,1,0:T(8,128)(2,1)S(1)}, bf16[1,1,3,128,128]{4,3,2,1,0:T(8,128)(2,1)}, u32[]{:S(2)}) copy-start(bf16[1,1,3,128,128]{4,3,2,1,0:T(8,128)(2,1)} %param.13) | copy-start | bytes 294916
  29.9 416.1 %all-reduce.3.cloned.1.call-start = ((), (), s32[]{:S(2)}) async-start(), calls=%async_computation.1 | async-start | bytes 262144
  177.8 5.1 collective-permute-start
  180.8 5.2 collective-permute-start.1
  187.4 0.7 copy-start.2
  542.4 5.4 collective-permute-start.2
  545.9 5.2 collective-permute-start.3
  714.3 5.4 collective-permute-start.4
  717.7 5.2 collective-permute-start.5
  892.9 5.6 collective-permute-start.6
  896.6 5.2 collective-permute-start.7
  1071.4 5.9 collective-permute-start.8
  1075.3 5.2 collective-permute-start.9
Sparse Core Ops, SparseCore 0:
  188.2 257.7 all-reduce.2
